TPU v7x, 32 devices: a whole 2x2x4 slice. The times are simulated.
32 devices in a mesh: rows: 8 (over y, x, core), chan: 4 (over z).
Axes of the slice: x: 2, y: 2, z: 4, core: 2. Of those that a mesh axis runs over, the one named last changes fastest.
Arguments:
- latents: bfloat16 [512, 4, 8, 128], P('chan', None, 'rows'), may hold values from -20 to 20
- cache_one: bfloat16 [512, 2, 8, 128], P('chan', None, 'rows'), may hold values from -4 to 4
- cache_two: bfloat16 [512, 2, 8, 128], P('chan', None, 'rows'), may hold values from -4 to 4
- gain_one: float32 [512], P('chan'), may hold values from 0.25 to 1.75
- bias_one: float32 [512], P('chan'), may hold values from -0.8 to 0.8
- weight_one: bfloat16 [3, 3, 3, 512, 512], P(None, None, None, None, 'chan'), may hold values from -0.0546875 to 0.0546875
- gain_two: float32 [512], P('chan'), may hold values from 0.25 to 1.75
- bias_two: float32 [512], P('chan'), may hold values from -0.8 to 0.8
- weight_two: bfloat16 [3, 3, 3, 512, 512], P(None, None, None, 'chan'), may hold values from -0.0625 to 0.0625
Outputs:
- upsampled: float32 [512, 4, 16, 256], P('chan', None, 'rows')
All inputs are finite; a program needn't handle non-finite values.
Results may differ from a plain program's by a relative error of at most 0.0022.
Values may be sent and summed in bfloat16 or wider, within the bound.
A program may use at most 64 MiB of HBM per device.

v0:
```python
import jax
import jax.numpy as jnp
from jax import lax
from jax.sharding import PartitionSpec as P

CHANNELS = 512
GROUPS = 32


epsilon = 1e-06


def padded(block, sides, width):
    for axis, dim in sides:
        count = lax.axis_size(axis)
        forward = [(i, i + 1) for i in range(count - 1)]
        backward = [(target, source) for source, target in forward]
        low = lax.ppermute(
            lax.slice_in_dim(block, block.shape[dim] - width, None, axis=dim), axis, forward
        )
        high = lax.ppermute(lax.slice_in_dim(block, 0, width, axis=dim), axis, backward)
        block = jnp.concatenate([low, block, high], axis=dim)
    return block


def group_silu(values, gain, bias):
    group_size = CHANNELS // GROUPS
    grouped = values.reshape(values.shape[0] // group_size, -1)
    sums, squares = lax.psum((jnp.sum(grouped, axis=1), jnp.sum(grouped * grouped, axis=1)), "rows")
    members = grouped.shape[1] * lax.axis_size("rows")
    average = sums / members
    spread = squares / members - average * average
    normed = ((grouped - average[:, None]) * lax.rsqrt(spread + epsilon)[:, None]).reshape(
        values.shape
    )
    scaled = normed * gain[:, None, None, None] + bias[:, None, None, None]
    return jax.nn.silu(scaled).astype(jnp.bfloat16)


def pad_rows(frames):
    return padded(frames, (("rows", 2),), 1)


def conv_block(frames, kernel):
    result = lax.conv_general_dilated(
        frames[None],
        kernel,
        (1, 1, 1),
        ((0, 0), (0, 0), (1, 1)),
        dimension_numbers=("NCDHW", "DHWIO", "NCDHW"),
        preferred_element_type=jnp.float32,
    )
    return result[0]


def gathered_conv(frames, kernel):
    initial = jnp.zeros(
        (kernel.shape[4], frames.shape[1] - 2, frames.shape[2] - 2, frames.shape[3]), jnp.float32
    )
    channels = lax.all_gather(frames, "chan", axis=0, tiled=True)
    section = lax.slice_in_dim(kernel, 0, channels.shape[0], axis=3)
    return initial + conv_block(channels, section)


def kernel_columns(kernel):
    return lax.all_to_all(kernel, "chan", split_axis=4, concat_axis=3, tiled=True)


def body(
    latents, cache_one, cache_two, gain_one, bias_one, weight_one, gain_two, bias_two, weight_two
):
    floats = latents.astype(jnp.float32)
    first = group_silu(floats, gain_one, bias_one)
    frames_one = pad_rows(jnp.concatenate([cache_one, first], axis=1))
    middle = gathered_conv(frames_one, weight_one).astype(jnp.bfloat16)
    second = group_silu(middle.astype(jnp.float32), gain_two, bias_two)
    frames_two = pad_rows(jnp.concatenate([cache_two, second], axis=1))
    columns = kernel_columns(weight_two)
    outcome = gathered_conv(frames_two, columns)
    result = floats + outcome
    return jnp.repeat(jnp.repeat(result, 2, axis=2), 2, axis=3)


def solution(mesh):
    return jax.shard_map(
        body,
        mesh=mesh,
        in_specs=(
            P("chan", None, "rows", None),
            P("chan", None, "rows", None),
            P("chan", None, "rows", None),
            P("chan"),
            P("chan"),
            P(None, None, None, None, "chan"),
            P("chan"),
            P("chan"),
            P(None, None, None, "chan", None),
        ),
        out_specs=P("chan", None, "rows", None),
        check_vma=False,
    )
```

profile of v0, /device:TPU:0, one launch (start us, length us, event | category | flops | bytes accessed | tf_op | source)
XLA Modules:
  0.0 272.5 jit_solution(15219196407137967923)
XLA Ops:
  6.5 1.2 convert_reduce_fusion
  8.1 15.6 %all-reduce.1 = (f32[8]{0:T(128)S(1)}, f32[8]{0:T(128)}) all-reduce(f32[8]{0:T(128)S(1)} %reduce_sum.54, f32[8]{0:T(128)S(1)} %reduce_sum.51), channel_id=1, replica_groups=mesh['rows'=8,'chan'=4] {'rows'}, use_global_device_ids=true, to_apply=%region_5.6 | all-reduce | flops 16 | bytes 128 | tf_op jit(solution)/shard_map/psum | solution.py:29
  26.7 1.3 collective-permute-start.1
  28.0 3.0 %collective-permute-start = (bf16[128,6,1,128]{3,0,2,1:T(8,128)(2,1)S(1)}, bf16[128,6,1,128]{3,0,2,1:T(8,128)(2,1)S(1)}, u32[]{:S(2)}, u32[]{:S(2)}) collective-permute-start(bf16[128,6,1,128]{3,0,2,1:T(8,128)(2,1)S(1)} %pad_maximum_fusion.2), channel_id=1, source_target_pairs={{0,4},{4,8},{8,12},{12,16},{16,20},{20,24},{24,28},{1,5},{5,9},{9,... | collective-permute-start | bytes 589832 | tf_op jit(solution)/shard_map/ppermute | solution.py:18
  33.0 8.1 %copy.53 = bf16[3,3,3,128,512]{3,2,1,0,4:T(4,128)(2,1)} copy(bf16[3,3,3,128,512]{4,3,2,1,0:T(8,128)(2,1)} %param.17) | data formatting | bytes 7077888 | tf_op args[8]
  41.1 5.0 %all-to-all-start = ((bf16[3,3,3,128,512]{3,2,1,0,4:T(4,128)(2,1)}), bf16[3,3,3,128,512]{3,2,1,0,4:T(4,128)(2,1)}, u32[]{:S(2)}, u32[]{:S(2)}) async-start(bf16[3,3,3,128,512]{3,2,1,0,4:T(4,128)(2,1)} %copy.53), calls=%async_computation | async-start | bytes 9437184 | tf_op jit(solution)/shard_map/all_to_all | solution.py:66
  46.2 84.4 %all-gather.3.cloned.1.call-done = bf16[512,6,3,128]{3,0,2,1:T(8,128)(2,1)} async-done(((bf16[128,6,3,128]{3,0,2,1:T(8,128)(2,1)}), bf16[512,6,3,128]{3,0,2,1:T(8,128)(2,1)}) %all-gather.3.cloned.1.call-update) | async-done | bytes 2359312 | tf_op jit(solution)/shard_map/all_gather | solution.py:60
  130.6 4.3 %copy.61 = bf16[512,6,3,1,128]{0,4,2,1,3:T(8,128)(2,1)} copy(bf16[512,6,3,1,128]{4,0,2,1,3:T(8,128)(2,1)} %bitcast.64) | data formatting | bytes 4718592
  134.9 4.1 %pad.clone = bf16[512,6,3,1,136]{0,4,2,1,3:T(8,128)(2,1)} pad(bf16[512,6,3,1,128]{0,4,2,1,3:T(8,128)(2,1)} %copy.61, bf16[]{:T(256)} %constant.17), padding=0_0x0_0x0_0x0_0x1_7 | pad | bytes 4866050 | tf_op jit(solution)/shard_map/broadcast_in_dim | solution.py:46
  139.0 5.0 %reshape.105 = bf16[512,6,3,1,8,17]{0,5,4,2,1,3:T(8,128)(2,1)} reshape(bf16[512,6,3,1,136]{0,4,2,1,3:T(8,128)(2,1)} %pad.clone) | data formatting | bytes 5013504 | tf_op jit(solution)/shard_map/conv_general_dilated | solution.py:45
  144.0 3.1 %copy.46 = bf16[512,6,3,1,8,17]{0,4,5,2,1,3:T(8,128)(2,1)S(1)} copy(bf16[512,6,3,1,8,17]{0,5,4,2,1,3:T(8,128)(2,1)} %reshape.105) | data formatting | bytes 5013504 | tf_op jit(solution)/shard_map/conv_general_dilated | solution.py:45
  147.1 4.7 %fusion.27 = (f32[128]{0:T(128)S(1)}, f32[128]{0:T(128)S(1)}, bf16[4,1,8,17,128]{4,2,3,1,0:T(8,128)(2,1)}) fusion(pred[8,17]{0,1:T(8,128)(4,1)S(1)} %copy-done.3, bf16[3,3,3,512,128]{4,3,2,1,0:T(8,128)(2,1)S(1)} %copy-done, bf16[512,6,3,1,7,2]{0,4,5,2,1,3:T(8,128)(2,1)S(1)} %slice.4, bf16[512,6,3,1,8,17]{0,4,5,2,1,3:T(8,128)(2,1)S(1)} %copy.46), kind=kOutput, calls=%fused_computation.28 | convolution fusion | flops 1934147328 | bytes 6444168 | tf_op jit(solution)/shard_map/conv_general_dilated | solution.py:45
  152.3 1.5 copy.49
  153.7 15.1 %all-reduce = (f32[8]{0:T(128)S(1)}, f32[8]{0:T(128)}) all-reduce(f32[8]{0:T(128)S(1)} %reduce_sum.75, f32[8]{0:T(128)S(1)} %reduce_sum.72), channel_id=1, replica_groups=mesh['rows'=8,'chan'=4] {'rows'}, use_global_device_ids=true, to_apply=%region_11.12 | all-reduce | flops 16 | bytes 128 | tf_op jit(solution)/shard_map/psum | solution.py:29
  170.5 1.7 copy.59
  175.1 1.3 collective-permute-start.3
  176.4 3.2 %collective-permute-start.2 = (bf16[128,6,1,128]{3,0,2,1:T(8,128)(2,1)S(1)}, bf16[128,6,1,128]{3,0,2,1:T(8,128)(2,1)S(1)}, u32[]{:S(2)}, u32[]{:S(2)}) collective-permute-start(bf16[128,6,1,128]{3,0,2,1:T(8,128)(2,1)S(1)} %pad_maximum_fusion.3), channel_id=1, source_target_pairs={{0,4},{4,8},{8,12},{12,16},{16,20},{20,24},{24,28},{1,5},{5,9},{9,... | collective-permute-start | bytes 589832 | tf_op jit(solution)/shard_map/ppermute | solution.py:18
  180.5 1.7 pad_maximum_fusion.1
  182.2 5.5 %all-to-all-done = bf16[3,3,3,128,512]{3,2,1,0,4:T(4,128)(2,1)} async-done(((bf16[3,3,3,128,512]{3,2,1,0,4:T(4,128)(2,1)}), bf16[3,3,3,128,512]{3,2,1,0,4:T(4,128)(2,1)}, u32[]{:S(2)}, u32[]{:S(2)}) %all-to-all-start) | async-done | bytes 3538976 | tf_op jit(solution)/shard_map/all_to_all | solution.py:66
  187.7 8.1 %copy.54 = bf16[3,3,3,128,4,128]{5,3,4,2,1,0:T(8,128)(2,1)} copy(bf16[3,3,3,128,4,128]{3,2,1,0,5,4:T(4,128)(2,1)} %bitcast.7) | data formatting | bytes 7077888 | tf_op jit(solution)/shard_map/all_to_all | solution.py:66
  195.7 36.8 %all-gather.5.cloned.1.call-done = bf16[512,6,3,128]{3,0,2,1:T(8,128)(2,1)} async-done(((bf16[128,6,3,128]{3,0,2,1:T(8,128)(2,1)}), bf16[512,6,3,128]{3,0,2,1:T(8,128)(2,1)}) %all-gather.5.cloned.1.call-update) | async-done | bytes 2359312 | tf_op jit(solution)/shard_map/all_gather | solution.py:60
  232.5 4.3 %copy.62 = bf16[512,6,3,1,128]{0,4,2,1,3:T(8,128)(2,1)} copy(bf16[512,6,3,1,128]{4,0,2,1,3:T(8,128)(2,1)} %bitcast.65) | data formatting | bytes 4718592
  236.8 4.1 %pad.2.clone = bf16[512,6,3,1,136]{0,4,2,1,3:T(8,128)(2,1)} pad(bf16[512,6,3,1,128]{0,4,2,1,3:T(8,128)(2,1)} %copy.62, bf16[]{:T(256)} %constant.17), padding=0_0x0_0x0_0x0_0x1_7 | pad | bytes 4866050 | tf_op jit(solution)/shard_map/broadcast_in_dim | solution.py:46
  240.9 5.0 %reshape.114 = bf16[512,6,3,1,8,17]{0,5,4,2,1,3:T(8,128)(2,1)} reshape(bf16[512,6,3,1,136]{0,4,2,1,3:T(8,128)(2,1)} %pad.2.clone) | data formatting | bytes 5013504 | tf_op jit(solution)/shard_map/conv_general_dilated | solution.py:45
  245.9 3.2 %copy.52 = bf16[512,6,3,1,8,17]{0,4,5,2,1,3:T(8,128)(2,1)S(1)} copy(bf16[512,6,3,1,8,17]{0,5,4,2,1,3:T(8,128)(2,1)} %reshape.114) | data formatting | bytes 5013504 | tf_op jit(solution)/shard_map/conv_general_dilated | solution.py:45
  249.2 4.0 %fusion.18 = f32[4,1,8,17,128]{4,2,3,1,0:T(8,128)S(1)} fusion(bf16[3,3,3,512,128]{4,3,2,1,0:T(8,128)(2,1)S(1)} %bitcast.63, bf16[512,6,3,1,7,2]{0,4,5,2,1,3:T(8,128)(2,1)S(1)} %slice.6, bf16[512,6,3,1,8,17]{0,4,5,2,1,3:T(8,128)(2,1)S(1)} %copy.52, pred[8,17]{0,1:T(8,128)(4,1)S(1)} %copy-done.4), kind=kOutput, calls=%fused_computation.17 | convolution fusion | flops 1933660160 | bytes 6582408 | tf_op jit(solution)/shard_map/conv_general_dilated | solution.py:45
  254.1 1.8 copy.60
  255.8 1.7 fusion.40
  257.5 1.8 copy.57
  259.3 1.9 broadcast_in_dim.24
  261.2 2.0 copy.58
  263.3 2.4 broadcast_in_dim.26
  (48 shorter events, 12.1 us)
Async XLA Ops:
  6.5 140.6 %copy-start = (bf16[3,3,3,512,128]{4,3,2,1,0:T(8,128)(2,1)S(1)}, bf16[3,3,3,512,128]{4,3,2,1,0:T(8,128)(2,1)}, u32[]{:S(2)}) copy-start(bf16[3,3,3,512,128]{4,3,2,1,0:T(8,128)(2,1)} %param.14) | copy-start | bytes 10616836
  6.5 124.1 %all-gather.3.cloned.1.call-start = ((), (), s32[]{:S(2)}) async-start(), calls=%async_computation.1 | async-start | bytes 2949120 | tf_op jit(solution)/shard_map/all_gather | solution.py:60
  26.7 4.4 %collective-permute-start.1 = (bf16[128,6,1,128]{3,0,2,1:T(8,128)(2,1)S(1)}, bf16[128,6,1,128]{3,0,2,1:T(8,128)(2,1)S(1)}, u32[]{:S(2)}, u32[]{:S(2)}) collective-permute-start(bf16[128,6,1,128]{3,0,2,1:T(8,128)(2,1)S(1)} %pad_maximum_fusion.2), channel_id=1, source_target_pairs={{4,0},{8,4},{12,8},{16,12},{20,16},{24,20},{28,24},{5,1},{9,5},{13... | collective-permute-start | bytes 589832 | tf_op jit(solution)/shard_map/ppermute | solution.py:21
  28.0 4.1 %collective-permute-start = (bf16[128,6,1,128]{3,0,2,1:T(8,128)(2,1)S(1)}, bf16[128,6,1,128]{3,0,2,1:T(8,128)(2,1)S(1)}, u32[]{:S(2)}, u32[]{:S(2)}) collective-permute-start(bf16[128,6,1,128]{3,0,2,1:T(8,128)(2,1)S(1)} %pad_maximum_fusion.2), channel_id=1, source_target_pairs={{0,4},{4,8},{8,12},{12,16},{16,20},{20,24},{24,28},{1,5},{5,9},{9,... | collective-permute-start | bytes 589832 | tf_op jit(solution)/shard_map/ppermute | solution.py:18
  41.1 146.5 %all-to-all-start = ((bf16[3,3,3,128,512]{3,2,1,0,4:T(4,128)(2,1)}), bf16[3,3,3,128,512]{3,2,1,0,4:T(4,128)(2,1)}, u32[]{:S(2)}, u32[]{:S(2)}) async-start(bf16[3,3,3,128,512]{3,2,1,0,4:T(4,128)(2,1)} %copy.53), calls=%async_computation | async-start | bytes 9437184 | tf_op jit(solution)/shard_map/all_to_all | solution.py:66
  46.1 186.4 %all-gather.5.cloned.1.call-start = ((), (), s32[]{:S(2)}) async-start(), calls=%async_computation.2 | async-start | bytes 2949120 | tf_op jit(solution)/shard_map/all_gather | solution.py:60
  144.0 3.2 %copy-start.3 = (pred[8,17]{0,1:T(8,128)(4,1)S(1)}, pred[8,17]{0,1:T(8,128)(4,1)}, u32[]{:S(2)}) copy-start(pred[8,17]{0,1:T(8,128)(4,1)} %constant.27) | copy-start | bytes 412
  147.1 26.0 %copy-start.2 = (f32[128]{0:T(128)S(1)}, f32[128]{0:T(128)}, u32[]{:S(2)}) copy-start(f32[128]{0:T(128)} %param.16) | copy-start | bytes 1540
  175.1 4.5 %collective-permute-start.3 = (bf16[128,6,1,128]{3,0,2,1:T(8,128)(2,1)S(1)}, bf16[128,6,1,128]{3,0,2,1:T(8,128)(2,1)S(1)}, u32[]{:S(2)}, u32[]{:S(2)}) collective-permute-start(bf16[128,6,1,128]{3,0,2,1:T(8,128)(2,1)S(1)} %pad_maximum_fusion.3), channel_id=1, source_target_pairs={{4,0},{8,4},{12,8},{16,12},{20,16},{24,20},{28,24},{5,1},{9,5},{13... | collective-permute-start | bytes 589832 | tf_op jit(solution)/shard_map/ppermute | solution.py:21
  176.4 4.1 %collective-permute-start.2 = (bf16[128,6,1,128]{3,0,2,1:T(8,128)(2,1)S(1)}, bf16[128,6,1,128]{3,0,2,1:T(8,128)(2,1)S(1)}, u32[]{:S(2)}, u32[]{:S(2)}) collective-permute-start(bf16[128,6,1,128]{3,0,2,1:T(8,128)(2,1)S(1)} %pad_maximum_fusion.3), channel_id=1, source_target_pairs={{0,4},{4,8},{8,12},{12,16},{16,20},{20,24},{24,28},{1,5},{5,9},{9,... | collective-permute-start | bytes 589832 | tf_op jit(solution)/shard_map/ppermute | solution.py:18
  245.9 3.3 %copy-start.1 = (bf16[3,3,3,128,4,128]{5,3,4,2,1,0:T(8,128)(2,1)S(1)}, bf16[3,3,3,128,4,128]{5,3,4,2,1,0:T(8,128)(2,1)}, u32[]{:S(2)}) copy-start(bf16[3,3,3,128,4,128]{5,3,4,2,1,0:T(8,128)(2,1)} %copy.54) | copy-start | bytes 10616836
  245.9 3.3 %copy-start.4 = (pred[8,17]{0,1:T(8,128)(4,1)S(1)}, pred[8,17]{0,1:T(8,128)(4,1)}, u32[]{:S(2)}) copy-start(pred[8,17]{0,1:T(8,128)(4,1)} %constant.27) | copy-start | bytes 412
Sparse Core Ops, SparseCore 0:
  33.1 97.4 all-gather.2
  182.3 50.1 all-gather.4
where the time goes:
time: 274 us; the launch traced here: 272 us
  waiting for transfers between devices  129 us (47%)
  local copies, waits for them, and re-layouts  66.6 us (24%)
  blocking collectives  30.7 us (11%)
  starting transfers between devices  13.9 us (5%)
  between operations  13.6 us (5%)
  other arithmetic  10.4 us (4%)
  matrix products  8.76 us (3%)
    all_gather x2, waiting for transfers between devices, gathered_conv(): channels = lax.all_gather(frames, 'chan', axis=0, tiled=True)  121 us
    psum x2, blocking collectives, group_silu(): lax.psum((jnp.sum(grouped, axis=1), jnp.sum(grouped * grouped, axis=1)),...  30.7 us
    unnamed x17, local copies, waits for them, and re-layouts  22.4 us
    conv_general_dilated x8, local copies, waits for them, and re-layouts, conv_block(): lax.conv_general_dilated(frames[None], kernel, (1, 1, 1), ((0, 0), (0, 0)...  17.2 us
    conv_general_dilated x2, matrix products, conv_block(): lax.conv_general_dilated(frames[None], kernel, (1, 1, 1), ((0, 0), (0, 0)...  8.76 us
    broadcast_in_dim x2, local copies, waits for them, and re-layouts, conv_block(): frames[None]  8.19 us
    all_to_all x1, local copies, waits for them, and re-layouts, kernel_columns(): lax.all_to_all(kernel, 'chan', split_axis=4, concat_axis=3, tiled=True)  8.07 us
    broadcast_in_dim x3, local copies, waits for them, and re-layouts, body(): return jnp.repeat(jnp.repeat(result, 2, axis=2), 2, axis=3)  6.32 us
  transfers between devices with their start and end apart: 7, of which 5 were waited for; matrix products, arithmetic and copies ran while one was open for 17% of the time, Pallas kernels for 0%

commit v1 on v0

--- a/solution.py
+++ b/solution.py
@@ -1,10 +1,17 @@
+import functools
+
 import jax
 import jax.numpy as jnp
 from jax import lax
+from jax.experimental import pallas as pl
+from jax.experimental.pallas import tpu as pltpu
 from jax.sharding import PartitionSpec as P
 
 CHANNELS = 512
 GROUPS = 32
+MESH = pl.DeviceIdType.MESH
+F32 = jnp.float32
+BF16 = jnp.bfloat16
 
 
 epsilon = 1e-06
@@ -54,19 +61,11 @@
 
 
 def gathered_conv(frames, kernel):
-    initial = jnp.zeros(
-        (kernel.shape[4], frames.shape[1] - 2, frames.shape[2] - 2, frames.shape[3]), jnp.float32
-    )
     channels = lax.all_gather(frames, "chan", axis=0, tiled=True)
-    section = lax.slice_in_dim(kernel, 0, channels.shape[0], axis=3)
-    return initial + conv_block(channels, section)
-
-
-def kernel_columns(kernel):
-    return lax.all_to_all(kernel, "chan", split_axis=4, concat_axis=3, tiled=True)
-
-
-def body(
+    return conv_block(channels, kernel)
+
+
+def plain_body(
     latents, cache_one, cache_two, gain_one, bias_one, weight_one, gain_two, bias_two, weight_two
 ):
     floats = latents.astype(jnp.float32)
@@ -75,10 +74,337 @@
     middle = gathered_conv(frames_one, weight_one).astype(jnp.bfloat16)
     second = group_silu(middle.astype(jnp.float32), gain_two, bias_two)
     frames_two = pad_rows(jnp.concatenate([cache_two, second], axis=1))
-    columns = kernel_columns(weight_two)
-    outcome = gathered_conv(frames_two, columns)
-    result = floats + outcome
+    columns = lax.all_to_all(weight_two, "chan", split_axis=4, concat_axis=3, tiled=True)
+    result = floats + gathered_conv(frames_two, columns)
     return jnp.repeat(jnp.repeat(result, 2, axis=2), 2, axis=3)
+
+
+def block_kernel(
+    R, Z, CL, T, W,
+    lat_ref, c1_ref, c2_ref, g1_ref, b1_ref, g2_ref, b2_ref, w1_hbm, w2_hbm,
+    out_ref,
+    tmp, lat_t, xa, xs1, acc1, part_out, part_in, mid, mid_in, x2, xs2, acc2,
+    st1, st2, rs_out, rs_in, w1, w2,
+    wsem, cs, cr, hs, hr, fs, fr, s1s, s1r, ps, pr, ms, mr, s2s, s2r, rss, rsr,
+):
+    row = lax.axis_index("rows")
+    me = lax.axis_index("chan")
+    M = T * W
+    C2 = 2 * W
+    has_up = row > 0
+    has_down = row < R - 1
+
+    barrier = pltpu.get_barrier_semaphore()
+    for k in range(1, R):
+        pl.semaphore_signal(barrier, inc=1, device_id={"rows": lax.rem(row + k, R)}, device_id_type=MESH)
+    for k in range(1, Z):
+        pl.semaphore_signal(barrier, inc=1, device_id={"chan": lax.rem(me + k, Z)}, device_id_type=MESH)
+
+    w_copies = []
+    for dt in range(3):
+        for dh in range(3):
+            w_copies.append(
+                pltpu.make_async_copy(
+                    w1_hbm.at[dt, dh], w1.at[dt, :, :, pl.ds(dh * CL, CL)], wsem.at[dt * 3 + dh]
+                )
+            )
+    w2_copy = pltpu.make_async_copy(w2_hbm, w2, wsem.at[9])
+    for copy in w_copies:
+        copy.start()
+    w2_copy.start()
+
+    def to_chan(src, dst, send, recv, k):
+        return pltpu.make_async_remote_copy(
+            src_ref=src, dst_ref=dst, send_sem=send, recv_sem=recv,
+            device_id={"chan": lax.rem(me + k, Z)}, device_id_type=MESH,
+        )
+
+    def to_row(src, dst, send, recv, k):
+        return pltpu.make_async_remote_copy(
+            src_ref=src, dst_ref=dst, send_sem=send, recv_sem=recv,
+            device_id={"rows": lax.rem(row + k, R)}, device_id_type=MESH,
+        )
+
+    tmp[0 : 2 * CL, :] = c1_ref[...].astype(F32)
+    for t in range(2):
+        xa[0, t * W : (t + 1) * W, :] = tmp[pl.ds(t, CL, stride=2), :].T.astype(BF16)
+    tmp[0 : 2 * CL, :] = c2_ref[...].astype(F32)
+    for t in range(2):
+        x2[1, t * W : (t + 1) * W, :] = tmp[pl.ds(t, CL, stride=2), :].T.astype(BF16)
+
+    pl.semaphore_wait(barrier, R - 1 + Z - 1)
+
+    caches = [
+        to_chan(xa.at[0, 0:C2], xa.at[k, 0:C2], cs.at[k], cr.at[k], k) for k in range(1, Z)
+    ]
+    for copy in caches:
+        copy.start()
+    halo_down = to_row(x2.at[1, 0:C2], x2.at[0, 0:C2], hs.at[0], hr.at[0], 1)
+    halo_up = to_row(x2.at[1, 0:C2], x2.at[2, 0:C2], hs.at[1], hr.at[1], R - 1)
+
+    tmp[...] = lat_ref[...].astype(F32)
+    for t in range(T):
+        lat_t[t * W : (t + 1) * W, :] = tmp[pl.ds(t, CL, stride=T), :].T
+
+    members = F32(R * M * (CHANNELS // GROUPS))
+    gi = lax.broadcasted_iota(jnp.int32, (CL, CL), 0) // (CHANNELS // GROUPS)
+    gj = lax.broadcasted_iota(jnp.int32, (CL, CL), 1) // (CHANNELS // GROUPS)
+    same_group = (gi == gj).astype(F32)
+
+    def share_stats(values, st, send, recv):
+        sums = jnp.sum(values, axis=0, keepdims=True)
+        squares = jnp.sum(values * values, axis=0, keepdims=True)
+        which = lax.broadcasted_iota(jnp.int32, (8, CL), 0)
+        st[0] = jnp.where(which == 0, sums, jnp.where(which == 1, squares, 0.0))
+        copies = [to_row(st.at[0], st.at[k], send.at[k], recv.at[k], k) for k in range(1, R)]
+        for copy in copies:
+            copy.start()
+        return copies
+
+    def finish_stats(copies, st, g_ref, b_ref):
+        for copy in copies:
+            copy.wait_recv()
+        total = st[0]
+        for k in range(1, R):
+            total = total + st[k]
+        total = jnp.dot(
+            total, same_group, preferred_element_type=F32, precision=lax.Precision.HIGHEST
+        ) / members
+        mean = total[0:1, :]
+        spread = jnp.maximum(total[1:2, :] - mean * mean, 0.0)
+        scale = lax.rsqrt(spread + epsilon) * g_ref[...]
+        return mean, scale, b_ref[...]
+
+    def normed(values, coefs):
+        mean, scale, bias = coefs
+        u = (values - mean) * scale + bias
+        return (u / (1.0 + jnp.exp(-u))).astype(BF16)
+
+    stats_one = share_stats(lat_t[...], st1, s1s, s1r)
+
+    @pl.when(has_down)
+    def _():
+        halo_down.start()
+
+    @pl.when(has_up)
+    def _():
+        halo_up.start()
+
+    coefs = finish_stats(stats_one, st1, g1_ref, b1_ref)
+    xa[0, C2:, :] = normed(lat_t[...], coefs)
+    firsts = [to_chan(xa.at[0, C2:], xa.at[k, C2:], fs.at[k], fr.at[k], k) for k in range(1, Z)]
+    for copy in firsts:
+        copy.start()
+
+    cell = lax.broadcasted_iota(jnp.int32, (C2 + M, CL), 0) % W
+
+    def shifted(block, store):
+        wide = block.astype(F32)
+        left = jnp.where(cell == 0, 0.0, pltpu.roll(wide, 1, 0)).astype(BF16)
+        right = jnp.where(cell == W - 1, 0.0, pltpu.roll(wide, C2 + M - 1, 0)).astype(BF16)
+        store(0, left)
+        store(1, block)
+        store(2, right)
+
+    for k in range(Z):
+        if k > 0:
+            caches[k - 1].wait_recv()
+            firsts[k - 1].wait_recv()
+        z = lax.rem(me - k + Z, Z)
+
+        def store_one(dx, value):
+            xs1[:, dx * CL : (dx + 1) * CL] = value
+
+        shifted(xa[k], store_one)
+        if k == 0:
+            for copy in w_copies:
+                copy.wait()
+        for dt in range(3):
+            base = pl.ds(pl.multiple_of(z * CL, CL), CL)
+            rhs = jnp.concatenate([w1[dt, dx, base, :] for dx in range(3)], axis=0)
+            term = jnp.dot(xs1[dt * W : dt * W + M, :], rhs, preferred_element_type=F32)
+            if k == 0 and dt == 0:
+                acc1[...] = term
+            else:
+                acc1[...] += term
+
+    part_down = to_row(part_out.at[0], part_in.at[0], ps.at[0], pr.at[0], 1)
+    part_up = to_row(part_out.at[1], part_in.at[1], ps.at[1], pr.at[1], R - 1)
+    part_out[0] = acc1[:, 0:CL].astype(part_out.dtype)
+
+    @pl.when(has_down)
+    def _():
+        part_down.start()
+
+    part_out[1] = acc1[:, 2 * CL : 3 * CL].astype(part_out.dtype)
+
+    @pl.when(has_up)
+    def _():
+        part_up.start()
+
+    acc1[:, 0:CL] = acc1[:, CL : 2 * CL]
+
+    @pl.when(has_up)
+    def _():
+        part_down.wait_recv()
+        acc1[:, 0:CL] += part_in[0].astype(F32)
+
+    @pl.when(has_down)
+    def _():
+        part_up.wait_recv()
+        acc1[:, 0:CL] += part_in[1].astype(F32)
+
+    mid[...] = acc1[:, 0:CL].astype(BF16)
+    mid_down = to_row(mid, mid_in.at[0], ms.at[0], mr.at[0], 1)
+    mid_up = to_row(mid, mid_in.at[1], ms.at[1], mr.at[1], R - 1)
+
+    stats_two = share_stats(mid[...].astype(F32), st2, s2s, s2r)
+
+    @pl.when(has_down)
+    def _():
+        mid_down.start()
+
+    @pl.when(has_up)
+    def _():
+        mid_up.start()
+
+    coefs_two = finish_stats(stats_two, st2, g2_ref, b2_ref)
+    w2_copy.wait()
+
+    def conv_two(dh, first):
+        def store_two(dx, value):
+            xs2[:, dx * CL : (dx + 1) * CL] = value
+
+        shifted(x2[dh], store_two)
+        for dt in range(3):
+            lhs = xs2[dt * W : dt * W + M, :]
+            term = jnp.dot(lhs, w2[dt, dh], preferred_element_type=F32)
+            for d in range(Z):
+                if first and dt == 0:
+                    acc2[d] = term[:, d * CL : (d + 1) * CL]
+                else:
+                    acc2[d] += term[:, d * CL : (d + 1) * CL]
+
+    x2[1, C2:, :] = normed(mid[...].astype(F32), coefs_two)
+    conv_two(1, True)
+
+    @pl.when(has_up)
+    def _():
+        halo_down.wait_recv()
+        mid_down.wait_recv()
+        x2[0, C2:, :] = normed(mid_in[0].astype(F32), coefs_two)
+        conv_two(0, False)
+
+    @pl.when(has_down)
+    def _():
+        halo_up.wait_recv()
+        mid_up.wait_recv()
+        x2[2, C2:, :] = normed(mid_in[1].astype(F32), coefs_two)
+        conv_two(2, False)
+
+    reduces = []
+    for k in range(1, Z):
+        rs_out[k - 1] = acc2[lax.rem(me + k, Z)].astype(rs_out.dtype)
+        copy = to_chan(rs_out.at[k - 1], rs_in.at[k - 1], rss.at[k], rsr.at[k], k)
+        copy.start()
+        reduces.append(copy)
+    lat_t[...] = lat_t[...] + acc2[me]
+    for k in range(1, Z):
+        reduces[k - 1].wait_recv()
+        lat_t[...] += rs_in[k - 1].astype(F32)
+
+    ei = lax.broadcasted_iota(jnp.int32, (W, 2 * W), 0)
+    ej = lax.broadcasted_iota(jnp.int32, (W, 2 * W), 1) // 2
+    twice = (ei == ej).astype(F32)
+    for t in range(T):
+        wide = jnp.dot(
+            lat_t[t * W : (t + 1) * W, :].T, twice,
+            preferred_element_type=F32, precision=lax.Precision.HIGHEST,
+        )
+        for half in range(2):
+            for again in range(2):
+                out_ref[pl.ds(t * 4 + half * 2 + again, CL, stride=4 * T), :] = wide[
+                    :, half * W : (half + 1) * W
+                ]
+
+    for copy in caches + firsts + stats_one + stats_two + reduces:
+        copy.wait_send()
+
+    @pl.when(has_down)
+    def _():
+        for copy in (halo_down, part_down, mid_down):
+            copy.wait_send()
+
+    @pl.when(has_up)
+    def _():
+        for copy in (halo_up, part_up, mid_up):
+            copy.wait_send()
+
+
+def body(
+    latents, cache_one, cache_two, gain_one, bias_one, weight_one, gain_two, bias_two, weight_two
+):
+    CL, T, rows_here, W = latents.shape
+    R, Z = lax.axis_size("rows"), lax.axis_size("chan")
+    if CL % 128 or W % 128 or rows_here != 1 or R < 2 or Z < 2:
+        return plain_body(
+            latents, cache_one, cache_two, gain_one, bias_one, weight_one, gain_two, bias_two,
+            weight_two,
+        )
+    C = CL * Z
+    M = T * W
+    vmem = pl.BlockSpec(memory_space=pltpu.VMEM)
+    anywhere = pl.BlockSpec(memory_space=pl.ANY)
+    dma = pltpu.SemaphoreType.DMA
+    out = pl.pallas_call(
+        functools.partial(block_kernel, R, Z, CL, T, W),
+        out_shape=jax.ShapeDtypeStruct((CL * T * 4, W), F32),
+        in_specs=[vmem] * 7 + [anywhere] * 2,
+        out_specs=vmem,
+        scratch_shapes=[
+            pltpu.VMEM((CL * T, W), F32),
+            pltpu.VMEM((M, CL), F32),
+            pltpu.VMEM((Z, M + 2 * W, CL), BF16),
+            pltpu.VMEM((M + 2 * W, 3 * CL), BF16),
+            pltpu.VMEM((M, 3 * CL), F32),
+            pltpu.VMEM((2, M, CL), BF16),
+            pltpu.VMEM((2, M, CL), BF16),
+            pltpu.VMEM((M, CL), BF16),
+            pltpu.VMEM((2, M, CL), BF16),
+            pltpu.VMEM((3, M + 2 * W, CL), BF16),
+            pltpu.VMEM((M + 2 * W, 3 * CL), BF16),
+            pltpu.VMEM((Z, M, CL), F32),
+            pltpu.VMEM((R, 8, CL), F32),
+            pltpu.VMEM((R, 8, CL), F32),
+            pltpu.VMEM((Z - 1, M, CL), BF16),
+            pltpu.VMEM((Z - 1, M, CL), BF16),
+            pltpu.VMEM((3, 3, C, 3 * CL), BF16),
+            pltpu.VMEM((3, 3, 3 * CL, C), BF16),
+            dma((10,)),
+            dma((Z,)), dma((Z,)),
+            dma((2,)), dma((2,)),
+            dma((Z,)), dma((Z,)),
+            dma((R,)), dma((R,)),
+            dma((2,)), dma((2,)),
+            dma((2,)), dma((2,)),
+            dma((R,)), dma((R,)),
+            dma((Z,)), dma((Z,)),
+        ],
+        compiler_params=pltpu.CompilerParams(
+            collective_id=0, has_side_effects=True, vmem_limit_bytes=40 * 1024 * 1024
+        ),
+    )(
+        latents.reshape(CL * T, W),
+        cache_one.reshape(CL * 2, W),
+        cache_two.reshape(CL * 2, W),
+        gain_one.reshape(1, CL),
+        bias_one.reshape(1, CL),
+        gain_two.reshape(1, CL),
+        bias_two.reshape(1, CL),
+        weight_one,
+        weight_two.reshape(3, 3, 3 * CL, C),
+    )
+    return out.reshape(CL, T, 2, 2, W).transpose(0, 1, 3, 2, 4).reshape(CL, T, 2, 2 * W)
 
 
 def solution(mesh):

time: 274 us -> 57.8 us (0.21)
  the two profiles are of different devices: /device:TPU:0 before, /device:TPU:10 now
where the time goes in v1:
time: 57.8 us; the launch traced here: 57.4 us
  Pallas kernels  47.2 us (82%)
  local copies, waits for them, and re-layouts  10.2 us (18%)
    pallas_call x1, Pallas kernels, body(): pl.pallas_call(functools.partial(block_kernel, R, Z, CL, T, W), out_shape...  47.2 us
    unnamed x19, local copies, waits for them, and re-layouts  10.2 us

profile of v1, /device:TPU:10, one launch (start us, length us, event | category | flops | bytes accessed | tf_op | source)
XLA Modules:
  0.0 57.4 jit_solution(6310307544263927328)
XLA Ops:
  0.0 0.0 copy-start
  0.0 2.0 %copy-done = bf16[3,3,3,512,128]{4,3,2,1,0:T(8,128)(2,1)S(1)} copy-done((bf16[3,3,3,512,128]{4,3,2,1,0:T(8,128)(2,1)S(1)}, bf16[3,3,3,512,128]{4,3,2,1,0:T(8,128)(2,1)}, u32[]{:S(2)}) %copy-start) | copy-done | bytes 3538968
  2.0 0.0 copy-start.1
  2.0 2.0 %copy-done.1 = bf16[3,3,3,128,512]{4,3,2,1,0:T(8,128)(2,1)S(1)} copy-done((bf16[3,3,3,128,512]{4,3,2,1,0:T(8,128)(2,1)S(1)}, bf16[3,3,3,128,512]{4,3,2,1,0:T(8,128)(2,1)}, u32[]{:S(2)}) %copy-start.1) | copy-done | bytes 3538968
  4.0 0.0 copy-start.2
  4.0 0.9 %copy-done.2 = bf16[128,4,1,128]{3,1,2,0:T(4,128)(2,1)S(1)} copy-done((bf16[128,4,1,128]{3,1,2,0:T(4,128)(2,1)S(1)}, bf16[128,4,1,128]{3,1,2,0:T(4,128)(2,1)}, u32[]{:S(2)}) %copy-start.2) | copy-done | bytes 131096
  4.9 0.0 copy-start.3
  4.9 0.8 %copy-done.3 = bf16[128,2,1,128]{3,1,2,0:T(2,128)(2,1)S(1)} copy-done((bf16[128,2,1,128]{3,1,2,0:T(2,128)(2,1)S(1)}, bf16[128,2,1,128]{3,1,2,0:T(2,128)(2,1)}, u32[]{:S(2)}) %copy-start.3) | copy-done | bytes 65560
  5.7 0.0 copy-start.4
  5.8 0.8 %copy-done.4 = bf16[128,2,1,128]{3,1,2,0:T(2,128)(2,1)S(1)} copy-done((bf16[128,2,1,128]{3,1,2,0:T(2,128)(2,1)S(1)}, bf16[128,2,1,128]{3,1,2,0:T(2,128)(2,1)}, u32[]{:S(2)}) %copy-start.4) | copy-done | bytes 65560
  6.6 0.0 copy-start.5
  6.6 0.7 %copy-done.5 = f32[128]{0:T(128)S(1)} copy-done((f32[128]{0:T(128)S(1)}, f32[128]{0:T(128)}, u32[]{:S(2)}) %copy-start.5) | copy-done | bytes 536
  7.2 0.0 copy-start.6
  7.2 0.7 %copy-done.6 = f32[128]{0:T(128)S(1)} copy-done((f32[128]{0:T(128)S(1)}, f32[128]{0:T(128)}, u32[]{:S(2)}) %copy-start.6) | copy-done | bytes 536
  7.9 0.0 copy-start.7
  7.9 0.7 %copy-done.7 = f32[128]{0:T(128)S(1)} copy-done((f32[128]{0:T(128)S(1)}, f32[128]{0:T(128)}, u32[]{:S(2)}) %copy-start.7) | copy-done | bytes 536
  8.6 0.0 copy-start.8
  8.6 0.7 %copy-done.8 = f32[128]{0:T(128)S(1)} copy-done((f32[128]{0:T(128)S(1)}, f32[128]{0:T(128)}, u32[]{:S(2)}) %copy-start.8) | copy-done | bytes 536
  9.2 47.2 %shard_map.91 = f32[2048,128]{1,0:T(8,128)S(1)} custom-call(bf16[512,128]{1,0:T(8,128)(2,1)S(1)} %bitcast.15, bf16[256,128]{1,0:T(8,128)(2,1)S(1)} %bitcast.16, bf16[256,128]{1,0:T(8,128)(2,1)S(1)} %bitcast.17, f32[1,128]{1,0:T(1,128)S(1)} %bitcast.18, f32[1,128]{1,0:T(1,128)S(1)} %bitcast.19, f32[1,128]{1,0:T(1,128)S(1)} %bitcast.20, ...), custom_call_target="tpu_custom_call" | custom-call | tf_op jit(solution)/shard_map/pallas_call | solution.py:359
  56.5 1.0 %copy.12 = f32[128,4,2,256]{3,2,1,0:T(2,128)} copy(f32[128,4,2,256]{3,2,1,0:T(2,128)S(1)} %bitcast.13) | data formatting | bytes 2097152
Async XLA Ops:
  0.0 2.0 %copy-start = (bf16[3,3,3,512,128]{4,3,2,1,0:T(8,128)(2,1)S(1)}, bf16[3,3,3,512,128]{4,3,2,1,0:T(8,128)(2,1)}, u32[]{:S(2)}) copy-start(bf16[3,3,3,512,128]{4,3,2,1,0:T(8,128)(2,1)} %w1_hbm.1) | copy-start | bytes 10616836
  2.0 2.0 %copy-start.1 = (bf16[3,3,3,128,512]{4,3,2,1,0:T(8,128)(2,1)S(1)}, bf16[3,3,3,128,512]{4,3,2,1,0:T(8,128)(2,1)}, u32[]{:S(2)}) copy-start(bf16[3,3,3,128,512]{4,3,2,1,0:T(8,128)(2,1)} %param.17) | copy-start | bytes 10616836
  4.0 0.9 %copy-start.2 = (bf16[128,4,1,128]{3,1,2,0:T(4,128)(2,1)S(1)}, bf16[128,4,1,128]{3,1,2,0:T(4,128)(2,1)}, u32[]{:S(2)}) copy-start(bf16[128,4,1,128]{3,1,2,0:T(4,128)(2,1)} %param.9) | copy-start | bytes 393220
  4.9 0.8 %copy-start.3 = (bf16[128,2,1,128]{3,1,2,0:T(2,128)(2,1)S(1)}, bf16[128,2,1,128]{3,1,2,0:T(2,128)(2,1)}, u32[]{:S(2)}) copy-start(bf16[128,2,1,128]{3,1,2,0:T(2,128)(2,1)} %param.10) | copy-start | bytes 196612
  5.7 0.8 %copy-start.4 = (bf16[128,2,1,128]{3,1,2,0:T(2,128)(2,1)S(1)}, bf16[128,2,1,128]{3,1,2,0:T(2,128)(2,1)}, u32[]{:S(2)}) copy-start(bf16[128,2,1,128]{3,1,2,0:T(2,128)(2,1)} %param.11) | copy-start | bytes 196612
  6.6 0.7 %copy-start.5 = (f32[128]{0:T(128)S(1)}, f32[128]{0:T(128)}, u32[]{:S(2)}) copy-start(f32[128]{0:T(128)} %param.12) | copy-start | bytes 1540
  7.2 0.7 %copy-start.6 = (f32[128]{0:T(128)S(1)}, f32[128]{0:T(128)}, u32[]{:S(2)}) copy-start(f32[128]{0:T(128)} %param.13) | copy-start | bytes 1540
  7.9 0.7 %copy-start.7 = (f32[128]{0:T(128)S(1)}, f32[128]{0:T(128)}, u32[]{:S(2)}) copy-start(f32[128]{0:T(128)} %param.15) | copy-start | bytes 1540
  8.6 0.7 %copy-start.8 = (f32[128]{0:T(128)S(1)}, f32[128]{0:T(128)}, u32[]{:S(2)}) copy-start(f32[128]{0:T(128)} %param.16) | copy-start | bytes 1540

commit v2 on v1

v2 whole, which is shorter than its diff:
```python
import functools

import jax
import jax.numpy as jnp
from jax import lax
from jax.experimental import pallas as pl
from jax.experimental.pallas import tpu as pltpu
from jax.sharding import PartitionSpec as P

CHANNELS = 512
GROUPS = 32
MESH = pl.DeviceIdType.MESH
F32 = jnp.float32
BF16 = jnp.bfloat16


epsilon = 1e-06


def padded(block, sides, width):
    for axis, dim in sides:
        count = lax.axis_size(axis)
        forward = [(i, i + 1) for i in range(count - 1)]
        backward = [(target, source) for source, target in forward]
        low = lax.ppermute(
            lax.slice_in_dim(block, block.shape[dim] - width, None, axis=dim), axis, forward
        )
        high = lax.ppermute(lax.slice_in_dim(block, 0, width, axis=dim), axis, backward)
        block = jnp.concatenate([low, block, high], axis=dim)
    return block


def group_silu(values, gain, bias):
    group_size = CHANNELS // GROUPS
    grouped = values.reshape(values.shape[0] // group_size, -1)
    sums, squares = lax.psum((jnp.sum(grouped, axis=1), jnp.sum(grouped * grouped, axis=1)), "rows")
    members = grouped.shape[1] * lax.axis_size("rows")
    average = sums / members
    spread = squares / members - average * average
    normed = ((grouped - average[:, None]) * lax.rsqrt(spread + epsilon)[:, None]).reshape(
        values.shape
    )
    scaled = normed * gain[:, None, None, None] + bias[:, None, None, None]
    return jax.nn.silu(scaled).astype(jnp.bfloat16)


def pad_rows(frames):
    return padded(frames, (("rows", 2),), 1)


def conv_block(frames, kernel):
    result = lax.conv_general_dilated(
        frames[None],
        kernel,
        (1, 1, 1),
        ((0, 0), (0, 0), (1, 1)),
        dimension_numbers=("NCDHW", "DHWIO", "NCDHW"),
        preferred_element_type=jnp.float32,
    )
    return result[0]


def gathered_conv(frames, kernel):
    channels = lax.all_gather(frames, "chan", axis=0, tiled=True)
    return conv_block(channels, kernel)


def plain_body(
    latents, cache_one, cache_two, gain_one, bias_one, weight_one, gain_two, bias_two, weight_two
):
    floats = latents.astype(jnp.float32)
    first = group_silu(floats, gain_one, bias_one)
    frames_one = pad_rows(jnp.concatenate([cache_one, first], axis=1))
    middle = gathered_conv(frames_one, weight_one).astype(jnp.bfloat16)
    second = group_silu(middle.astype(jnp.float32), gain_two, bias_two)
    frames_two = pad_rows(jnp.concatenate([cache_two, second], axis=1))
    columns = lax.all_to_all(weight_two, "chan", split_axis=4, concat_axis=3, tiled=True)
    result = floats + gathered_conv(frames_two, columns)
    return jnp.repeat(jnp.repeat(result, 2, axis=2), 2, axis=3)


def block_kernel(
    R, Z, CL, T, W,
    lat_hbm, c1_hbm, c2_hbm, g1_hbm, b1_hbm, g2_hbm, b2_hbm, w1_hbm, w2_hbm,
    out_ref,
    lat_v, c1_v, c2_v, g1, b1, g2, b2,
    tmp, lat_t, xa, xs1, acc1, part_out, part_in, mid, mid_in, x2, xs2, acc2,
    st1, st2, rs_out, rs_in, w1, w2,
    isem, wsem, cs, cr, hs, hr, fs, fr, s1s, s1r, ps, pr, ms, mr, s2s, s2r, rss, rsr,
):
    row = lax.axis_index("rows")
    me = lax.axis_index("chan")
    M = T * W
    C2 = 2 * W
    ZH = Z // 2
    H = M // 2
    has_up = row > 0
    has_down = row < R - 1

    def partner(k):
        other = me * 0
        bit = 1
        while bit < Z:
            mine = (me // bit) % 2
            other = other + bit * ((1 - mine) if k & bit else mine)
            bit *= 2
        return other

    barrier = pltpu.get_barrier_semaphore()
    for k in range(1, R):
        pl.semaphore_signal(barrier, inc=1, device_id={"rows": lax.rem(row + k, R)}, device_id_type=MESH)
    for k in range(1, Z):
        pl.semaphore_signal(barrier, inc=1, device_id={"chan": partner(k)}, device_id_type=MESH)

    loads = [
        pltpu.make_async_copy(src, dst, isem.at[i])
        for i, (src, dst) in enumerate(
            [
                (lat_hbm, lat_v), (c1_hbm, c1_v), (c2_hbm, c2_v),
                (g1_hbm, g1), (b1_hbm, b1), (g2_hbm, g2), (b2_hbm, b2),
            ]
        )
    ]
    place = (0, 2, 1)
    w_copies = []
    for dt in range(3):
        for dh in range(3):
            w_copies.append(
                pltpu.make_async_copy(
                    w1_hbm.at[dt, dh],
                    w1.at[dt, :, :, pl.ds(place[dh] * CL, CL)],
                    wsem.at[dt * 3 + dh],
                )
            )
    w2_copy = pltpu.make_async_copy(w2_hbm, w2, wsem.at[9])
    for copy in loads + w_copies + [w2_copy]:
        copy.start()

    def to_chan(src, dst, send, recv, k):
        return pltpu.make_async_remote_copy(
            src_ref=src, dst_ref=dst, send_sem=send, recv_sem=recv,
            device_id={"chan": partner(k)}, device_id_type=MESH,
        )

    def to_row(src, dst, send, recv, k):
        return pltpu.make_async_remote_copy(
            src_ref=src, dst_ref=dst, send_sem=send, recv_sem=recv,
            device_id={"rows": lax.rem(row + k, R)}, device_id_type=MESH,
        )

    members = F32(R * M * (CHANNELS // GROUPS))
    gi = lax.broadcasted_iota(jnp.int32, (CL, CL), 0) // (CHANNELS // GROUPS)
    gj = lax.broadcasted_iota(jnp.int32, (CL, CL), 1) // (CHANNELS // GROUPS)
    same_group = (gi == gj).astype(F32)

    def share_stats(values, st, send, recv):
        sums = jnp.sum(values, axis=0, keepdims=True)
        squares = jnp.sum(values * values, axis=0, keepdims=True)
        which = lax.broadcasted_iota(jnp.int32, (8, CL), 0)
        st[0] = jnp.where(which == 0, sums, jnp.where(which == 1, squares, 0.0))
        copies = [to_row(st.at[0], st.at[k], send.at[k], recv.at[k], k) for k in range(1, R)]
        for copy in copies:
            copy.start()
        return copies

    def finish_stats(copies, st, g_ref, b_ref):
        for copy in copies:
            copy.wait_recv()
        total = st[0]
        for k in range(1, R):
            total = total + st[k]
        total = jnp.dot(
            total, same_group, preferred_element_type=F32, precision=lax.Precision.HIGHEST
        ) / members
        mean = total[0:1, :]
        spread = jnp.maximum(total[1:2, :] - mean * mean, 0.0)
        scale = lax.rsqrt(spread + epsilon) * g_ref[...]
        return mean, scale, b_ref[...]

    def normed(values, coefs):
        mean, scale, bias = coefs
        u = (values - mean) * scale + bias
        return (u / (1.0 + jnp.exp(-u))).astype(BF16)

    def shifted(block):
        rows = block.shape[0]
        cell = lax.broadcasted_iota(jnp.int32, (rows, CL), 0) % W
        wide = block.astype(F32)
        left = jnp.where(cell == 0, 0.0, pltpu.roll(wide, 1, 0)).astype(BF16)
        right = jnp.where(cell == W - 1, 0.0, pltpu.roll(wide, rows - 1, 0)).astype(BF16)
        return left, block, right

    loads[0].wait()
    tmp[...] = lat_v[...].astype(F32)
    for t in range(T):
        lat_t[t * W : (t + 1) * W, :] = tmp[pl.ds(t, CL, stride=T), :].T
    loads[1].wait()
    tmp[0 : 2 * CL, :] = c1_v[...].astype(F32)
    for t in range(2):
        xa[0, t * W : (t + 1) * W, :] = tmp[pl.ds(t, CL, stride=2), :].T.astype(BF16)

    pl.semaphore_wait(barrier, R - 1 + Z - 1)

    stats_one = share_stats(lat_t[...], st1, s1s, s1r)
    caches = [
        to_chan(xa.at[0, 0:C2], xa.at[k, 0:C2], cs.at[k], cr.at[k], k) for k in range(1, Z)
    ]
    for copy in caches[::-1]:
        copy.start()

    loads[2].wait()
    tmp[0 : 2 * CL, :] = c2_v[...].astype(F32)
    for t in range(2):
        x2[1, t * W : (t + 1) * W, :] = tmp[pl.ds(t, CL, stride=2), :].T.astype(BF16)
    halo_down = to_row(x2.at[1], x2.at[0], hs.at[0], hr.at[0], 1)
    halo_up = to_row(x2.at[1], x2.at[2], hs.at[1], hr.at[1], R - 1)

    @pl.when(has_down)
    def _():
        halo_down.start()

    @pl.when(has_up)
    def _():
        halo_up.start()

    for copy in loads[3:]:
        copy.wait()
    coefs = finish_stats(stats_one, st1, g1, b1)
    xa[0, C2:, :] = normed(lat_t[...], coefs)
    firsts = [to_chan(xa.at[0, C2:], xa.at[k, C2:], fs.at[k], fr.at[k], k) for k in range(1, Z)]
    for copy in firsts[::-1]:
        copy.start()

    part_down = to_row(part_out.at[0], part_in.at[0], ps.at[0], pr.at[0], 1)
    part_up = to_row(part_out.at[1], part_in.at[1], ps.at[1], pr.at[1], R - 1)

    def kernel_one(dt, z, low, high):
        base = pl.ds(pl.multiple_of(z * CL, CL), CL)
        return jnp.concatenate([w1[dt, dx, base, low:high] for dx in range(3)], axis=0)

    for copy in w_copies:
        copy.wait()
    for k in range(Z):
        if k > 0:
            caches[k - 1].wait_recv()
            firsts[k - 1].wait_recv()
        z = partner(k)
        for dx, value in enumerate(shifted(xa[k])):
            xs1[:, dx * CL : (dx + 1) * CL] = value
        parts = ((0, 2 * CL), (2 * CL, 3 * CL)) if k == Z - 1 else ((0, 3 * CL),)
        for low, high in parts:
            for dt in range(3):
                term = jnp.dot(
                    xs1[dt * W : dt * W + M, :], kernel_one(dt, z, low, high),
                    preferred_element_type=F32,
                )
                if k == 0 and dt == 0:
                    acc1[:, low:high] = term
                else:
                    acc1[:, low:high] += term
            if k == Z - 1 and low == 0:
                part_out[0] = acc1[:, 0:CL].astype(part_out.dtype)
                part_out[1] = acc1[:, CL : 2 * CL].astype(part_out.dtype)

                @pl.when(has_down)
                def _():
                    part_down.start()

                @pl.when(has_up)
                def _():
                    part_up.start()

        if k == 0:
            w2_copy.wait()

            @pl.when(has_up)
            def _():
                halo_down.wait_recv()

            @pl.when(has_down)
            def _():
                halo_up.wait_recv()

            @pl.when(jnp.logical_not(has_up))
            def _():
                x2[0] = jnp.zeros((C2, CL), BF16)

            @pl.when(jnp.logical_not(has_down))
            def _():
                x2[2] = jnp.zeros((C2, CL), BF16)

            for dh in range(3):
                for dx, value in enumerate(shifted(x2[dh])):
                    xs2[0:C2, (dh * 3 + dx) * CL : (dh * 3 + dx + 1) * CL] = value
            both = jnp.dot(xs2[0:C2, :], w2[0], preferred_element_type=F32)
            one = jnp.dot(xs2[W:C2, :], w2[1], preferred_element_type=F32)
            for d in range(Z):
                cols = slice(d * CL, (d + 1) * CL)
                acc2[d, 0:W] = both[0:W, cols] + one[:, cols]
                acc2[d, W:C2] = both[W:C2, cols]
                acc2[d, C2:] = jnp.zeros((M - C2, CL), F32)

    @pl.when(has_up)
    def _():
        part_down.wait_recv()
        acc1[:, 2 * CL :] += part_in[0].astype(F32)

    @pl.when(has_down)
    def _():
        part_up.wait_recv()
        acc1[:, 2 * CL :] += part_in[1].astype(F32)

    mid[...] = acc1[:, 2 * CL :].astype(BF16)
    mid_down = to_row(mid, mid_in.at[0], ms.at[0], mr.at[0], 1)
    mid_up = to_row(mid, mid_in.at[1], ms.at[1], mr.at[1], R - 1)

    @pl.when(has_down)
    def _():
        mid_down.start()

    @pl.when(has_up)
    def _():
        mid_up.start()

    stats_two = share_stats(mid[...].astype(F32), st2, s2s, s2r)
    coefs_two = finish_stats(stats_two, st2, g2, b2)

    def place_row(dh, values):
        for dx, value in enumerate(shifted(normed(values.astype(F32), coefs_two))):
            xs2[C2:, (dh * 3 + dx) * CL : (dh * 3 + dx + 1) * CL] = value

    place_row(1, mid[...])

    @pl.when(has_up)
    def _():
        mid_down.wait_recv()
        place_row(0, mid_in[0])

    @pl.when(has_down)
    def _():
        mid_up.wait_recv()
        place_row(2, mid_in[1])

    @pl.when(jnp.logical_not(has_up))
    def _():
        xs2[C2:, 0 : 3 * CL] = jnp.zeros((M, 3 * CL), BF16)

    @pl.when(jnp.logical_not(has_down))
    def _():
        xs2[C2:, 6 * CL :] = jnp.zeros((M, 3 * CL), BF16)

    mine = me // ZH
    reduces = {}
    for turn in range(2):
        half = 1 - mine if turn == 0 else mine
        cols = pl.ds(pl.multiple_of(half * (ZH * CL), ZH * CL), ZH * CL)
        for dt in (2, 1, 0):
            start = C2 - dt * W
            term = jnp.dot(
                xs2[C2 : C2 + M - start, :], w2[dt, :, cols], preferred_element_type=F32
            )
            for j in range(ZH):
                acc2[half * ZH + j, start:] += term[:, j * CL : (j + 1) * CL]
        ks = range(ZH, Z) if turn == 0 else range(1, ZH)
        for f in range(2):
            rows = slice(f * H, (f + 1) * H)
            for k in ks:
                rs_out[k - 1, rows] = acc2[partner(k), rows].astype(rs_out.dtype)
                copy = to_chan(
                    rs_out.at[k - 1, rows], rs_in.at[k - 1, rows], rss.at[f, k], rsr.at[f, k], k
                )
                copy.start()
                reduces[f, k] = copy
    lat_t[...] = lat_t[...] + acc2[me]

    ei = lax.broadcasted_iota(jnp.int32, (W, 2 * W), 0)
    ej = lax.broadcasted_iota(jnp.int32, (W, 2 * W), 1) // 2
    twice = (ei == ej).astype(F32)
    for f in range(2):
        for k in range(1, Z):
            reduces[f, k].wait_recv()
        for t in range(f * T // 2, (f + 1) * T // 2):
            rows = slice(t * W, (t + 1) * W)
            total = lat_t[rows, :]
            for k in range(1, Z):
                total = total + rs_in[k - 1, rows].astype(F32)
            wide = jnp.dot(
                total.T, twice, preferred_element_type=F32, precision=lax.Precision.HIGHEST
            )
            for side in range(2):
                for again in range(2):
                    out_ref[pl.ds(t * 4 + side * 2 + again, CL, stride=4 * T), :] = wide[
                        :, side * W : (side + 1) * W
                    ]

    for copy in caches + firsts + stats_one + stats_two + list(reduces.values()):
        copy.wait_send()

    @pl.when(has_down)
    def _():
        for copy in (halo_down, part_down, mid_down):
            copy.wait_send()

    @pl.when(has_up)
    def _():
        for copy in (halo_up, part_up, mid_up):
            copy.wait_send()


def body(
    latents, cache_one, cache_two, gain_one, bias_one, weight_one, gain_two, bias_two, weight_two
):
    CL, T, rows_here, W = latents.shape
    R, Z = lax.axis_size("rows"), lax.axis_size("chan")
    if CL % 128 or W % 128 or rows_here != 1 or T % 2 or R < 2 or Z < 2 or Z & (Z - 1):
        return plain_body(
            latents, cache_one, cache_two, gain_one, bias_one, weight_one, gain_two, bias_two,
            weight_two,
        )
    C = CL * Z
    M = T * W
    vmem = pl.BlockSpec(memory_space=pltpu.VMEM)
    hbm = pl.BlockSpec(memory_space=pltpu.HBM)
    dma = pltpu.SemaphoreType.DMA
    out = pl.pallas_call(
        functools.partial(block_kernel, R, Z, CL, T, W),
        out_shape=jax.ShapeDtypeStruct((CL * T * 4, W), F32),
        in_specs=[hbm] * 9,
        out_specs=vmem,
        scratch_shapes=[
            pltpu.VMEM((CL * T, W), BF16),
            pltpu.VMEM((CL * 2, W), BF16),
            pltpu.VMEM((CL * 2, W), BF16),
            pltpu.VMEM((1, CL), F32),
            pltpu.VMEM((1, CL), F32),
            pltpu.VMEM((1, CL), F32),
            pltpu.VMEM((1, CL), F32),
            pltpu.VMEM((CL * T, W), F32),
            pltpu.VMEM((M, CL), F32),
            pltpu.VMEM((Z, M + 2 * W, CL), BF16),
            pltpu.VMEM((M + 2 * W, 3 * CL), BF16),
            pltpu.VMEM((M, 3 * CL), F32),
            pltpu.VMEM((2, M, CL), BF16),
            pltpu.VMEM((2, M, CL), BF16),
            pltpu.VMEM((M, CL), BF16),
            pltpu.VMEM((2, M, CL), BF16),
            pltpu.VMEM((3, 2 * W, CL), BF16),
            pltpu.VMEM((M + 2 * W, 9 * CL), BF16),
            pltpu.VMEM((Z, M, CL), F32),
            pltpu.VMEM((R, 8, CL), F32),
            pltpu.VMEM((R, 8, CL), F32),
            pltpu.VMEM((Z - 1, M, CL), BF16),
            pltpu.VMEM((Z - 1, M, CL), BF16),
            pltpu.VMEM((3, 3, C, 3 * CL), BF16),
            pltpu.VMEM((3, 9 * CL, C), BF16),
            dma((7,)),
            dma((10,)),
            dma((Z,)), dma((Z,)),
            dma((2,)), dma((2,)),
            dma((Z,)), dma((Z,)),
            dma((R,)), dma((R,)),
            dma((2,)), dma((2,)),
            dma((2,)), dma((2,)),
            dma((R,)), dma((R,)),
            dma((2, Z)), dma((2, Z)),
        ],
        compiler_params=pltpu.CompilerParams(
            collective_id=0, has_side_effects=True, vmem_limit_bytes=60 * 1024 * 1024
        ),
    )(
        latents.reshape(CL * T, W),
        cache_one.reshape(CL * 2, W),
        cache_two.reshape(CL * 2, W),
        gain_one.reshape(1, CL),
        bias_one.reshape(1, CL),
        gain_two.reshape(1, CL),
        bias_two.reshape(1, CL),
        weight_one,
        weight_two.reshape(3, 9 * CL, C),
    )
    return out.reshape(CL, T, 2, 2, W).transpose(0, 1, 3, 2, 4).reshape(CL, T, 2, 2 * W)


def solution(mesh):
    return jax.shard_map(
        body,
        mesh=mesh,
        in_specs=(
            P("chan", None, "rows", None),
            P("chan", None, "rows", None),
            P("chan", None, "rows", None),
            P("chan"),
            P("chan"),
            P(None, None, None, None, "chan"),
            P("chan"),
            P("chan"),
            P(None, None, None, "chan", None),
        ),
        out_specs=P("chan", None, "rows", None),
        check_vma=False,
    )
```

time: 57.8 us -> 52 us (0.90)
  the two profiles are of different devices: /device:TPU:10 before, /device:TPU:0 now
where the time goes in v2:
time: 52 us; the launch traced here: 51.8 us
  Pallas kernels  49.3 us (95%)
  local copies, waits for them, and re-layouts  2.55 us (5%)
    pallas_call x1, Pallas kernels, body(): pl.pallas_call(functools.partial(block_kernel, R, Z, CL, T, W), out_shape...  49.3 us
    unnamed x1, local copies, waits for them, and re-layouts  2.55 us

profile of v2, /device:TPU:0, one launch (start us, length us, event | category | flops | bytes accessed | tf_op | source)
XLA Modules:
  0.0 51.8 jit_solution(17571801247352570035)
XLA Ops:
  0.0 49.3 %shard_map.91 = f32[2048,128]{1,0:T(8,128)} custom-call(bf16[512,128]{1,0:T(8,128)(2,1)} %bitcast.15, bf16[256,128]{1,0:T(8,128)(2,1)} %bitcast.16, bf16[256,128]{1,0:T(8,128)(2,1)} %bitcast.17, f32[1,128]{1,0:T(1,128)} %bitcast.18, f32[1,128]{1,0:T(1,128)} %bitcast.19, f32[1,128]{1,0:T(1,128)} %bitcast.20, f32[1,128]{1,0:T(1,128)} %bitcast.21, ...), custom_call_target="tpu_custom_call" | custom-call | tf_op jit(solution)/shard_map/pallas_call | solution.py:425
  49.3 2.6 %copy.12 = f32[128,4,2,256]{3,2,1,0:T(2,128)} copy(f32[128,4,2,256]{3,2,1,0:T(2,128)} %bitcast.13) | data formatting | bytes 2097152

commit v3 on v2

--- a/solution.py
+++ b/solution.py
@@ -465,9 +465,9 @@
             dma((2, Z)), dma((2, Z)),
         ],
         compiler_params=pltpu.CompilerParams(
-            collective_id=0, has_side_effects=True, vmem_limit_bytes=60 * 1024 * 1024
+            collective_id=0, has_side_effects=True, vmem_limit_bytes=40 * 1024 * 1024
         ),
-    )(
+    )(*(pltpu.with_memory_space_constraint(v, pltpu.HBM) for v in (
         latents.reshape(CL * T, W),
         cache_one.reshape(CL * 2, W),
         cache_two.reshape(CL * 2, W),
@@ -477,7 +477,7 @@
         bias_two.reshape(1, CL),
         weight_one,
         weight_two.reshape(3, 9 * CL, C),
-    )
+    )))
     return out.reshape(CL, T, 2, 2, W).transpose(0, 1, 3, 2, 4).reshape(CL, T, 2, 2 * W)
 
 

time: 52 us -> 49.4 us (0.950)
  local copies, waits for them, and re-layouts: 2.55 us -> 0.97 us
  Pallas kernels: 49.3 us -> 48.3 us
    unnamed x1, local copies, waits for them, and re-layouts: 2.55 us -> 0.97 us
    pallas_call x1, Pallas kernels: 49.3 us -> 48.3 us  [body(): pl.pallas_call(functools.partial(block_kernel, R, Z, CL, T, W), out_shape...]
where the time goes in v3:
time: 49.4 us; the launch traced here: 49.3 us
  Pallas kernels  48.3 us (98%)
  local copies, waits for them, and re-layouts  0.97 us (2%)
    pallas_call x1, Pallas kernels, body(): pl.pallas_call(functools.partial(block_kernel, R, Z, CL, T, W), out_shape...  48.3 us

profile of v3, /device:TPU:0, one launch (start us, length us, event | category | flops | bytes accessed | tf_op | source)
XLA Modules:
  0.0 49.3 jit_solution(7137821932077855072)
XLA Ops:
  0.0 48.3 %shard_map.91 = f32[2048,128]{1,0:T(8,128)S(1)} custom-call(bf16[512,128]{1,0:T(8,128)(2,1)} %bitcast.15, bf16[256,128]{1,0:T(8,128)(2,1)} %bitcast.16, bf16[256,128]{1,0:T(8,128)(2,1)} %bitcast.17, f32[1,128]{1,0:T(1,128)} %bitcast.18, f32[1,128]{1,0:T(1,128)} %bitcast.19, f32[1,128]{1,0:T(1,128)} %bitcast.20, f32[1,128]{1,0:T(1,128)} %bitcast.21, ...), custom_call_target="tpu_custom_call" | custom-call | tf_op jit(solution)/shard_map/pallas_call | solution.py:425
  48.3 1.0 %copy.12 = f32[128,4,2,256]{3,2,1,0:T(2,128)} copy(f32[128,4,2,256]{3,2,1,0:T(2,128)S(1)} %bitcast.13) | data formatting | bytes 2097152
